TPU v7x, 256 devices: a whole 4x4x8 slice. The times are simulated.
256 devices in a mesh: dp: 64 (over y, z, x_lo), fsdp: 4 (over x_hi, core).
Axes of the slice: x: 4 (x_hi: 2, x_lo: 2; x = x_hi * 2 + x_lo), y: 4, z: 8, core: 2. Of those that a mesh axis runs over, the one named last changes fastest.
Arguments:
- picture_tower_inputs: bfloat16 [131072, 1152], P(('dp', 'fsdp')), may hold values from -6 to 6
- caption_tower_inputs: bfloat16 [131072, 1152], P(('dp', 'fsdp')), may hold values from -6 to 6
- halfwidth_parameter_matrix: bfloat16 [1152, 2304], P('fsdp'), may hold values from -0.1875 to 0.1875
- affinity_multiplier: float32 [1], replicated, may hold values from 4 to 12
- affinity_offset: float32 [1], replicated, may hold values from -6 to -2
- precise_parameter_copy: float32 [1152, 2304], P('fsdp', 'dp'), may hold values from -0.125 to 0.125
- gradient_mean_estimate: float32 [1152, 2304], P('fsdp', 'dp'), may hold values from -4 to 4
- gradient_variance_estimate: float32 [1152, 2304], P('fsdp', 'dp'), may hold values from 0.05 to 1
Outputs:
- img_tangent: bfloat16 [131072, 1152], P(('dp', 'fsdp'))
- txt_tangent: bfloat16 [131072, 1152], P(('dp', 'fsdp'))
- new_master: float32 [1152, 2304], P('fsdp', 'dp')
- new_one: float32 [1152, 2304], P('fsdp', 'dp')
- new_two: float32 [1152, 2304], P('fsdp', 'dp')
- new_weights: bfloat16 [1152, 2304], P('fsdp')
All inputs are finite; a program needn't handle non-finite values.
Results may differ from a plain program's by a relative error of at most 0.008.
Values may be sent and summed in bfloat16 or wider, within the bound.
No kernel may reach another device: no remote copies, remote signals or barrier semaphores. Data moves between devices by JAX's collectives and lax.ppermute only.
A program may use at most 128 MiB of HBM per device.

v0:
```python
import jax
import jax.numpy as jnp
from jax import lax
from jax.sharding import PartitionSpec as P

CYCLE = 4


def shifted(value, axis, steps):
    count = lax.axis_size(axis)
    pairs = [(source, (source + steps) % count) for source in range(count)]
    return lax.ppermute(value, axis, pairs)


def normalize(projected):
    inv_norm = lax.rsqrt(jnp.sum(projected * projected, axis=-1, keepdims=True) + 1e-06)
    return (projected * inv_norm, inv_norm)


def contract_rows(left, right):
    return lax.dot_general(
        left, right, (((0,), (0,)), ((), ())), preferred_element_type=jnp.float32
    )


def weigh_pairs(image_rows, text_rows, affinity_multiplier_name, shift_value, sign_label):
    logits = (
        affinity_multiplier_name
        * lax.dot_general(
            image_rows, text_rows, (((1,), (1,)), ((), ())), preferred_element_type=jnp.float32
        )
        + shift_value
    )
    return (-sign_label * jax.nn.sigmoid(-sign_label * logits) * affinity_multiplier_name).astype(
        jnp.bfloat16
    )


def body(
    picture_tower_inputs,
    caption_tower_inputs,
    halfwidth_parameter_matrix,
    affinity_multiplier,
    affinity_offset,
    precise_parameter_copy,
    gradient_mean_estimate,
    gradient_variance_estimate,
):
    row_count = picture_tower_inputs.shape[0]
    feature_width = picture_tower_inputs.shape[1]
    zero_block = jnp.zeros((row_count, feature_width), jnp.float32)
    rows_per_block = lax.all_gather(halfwidth_parameter_matrix, "fsdp", axis=0, tiled=True)
    part_img = picture_tower_inputs
    part_txt = caption_tower_inputs
    proj_img = jnp.dot(
        part_img, rows_per_block[:, :feature_width], preferred_element_type=jnp.float32
    )
    proj_txt = jnp.dot(
        part_txt, rows_per_block[:, feature_width:], preferred_element_type=jnp.float32
    )
    unit_img, norm_img = normalize(proj_img)
    normalized_text, norm_txt = normalize(proj_txt)
    low_img = unit_img.astype(jnp.bfloat16)
    low_txt = normalized_text.astype(jnp.bfloat16)
    affinity_multiplier_name = affinity_multiplier[0]
    shift_value = affinity_offset[0]
    identity_mask = jnp.eye(row_count, dtype=jnp.float32)
    negative_label = -jnp.ones_like(identity_mask)
    visiting = low_txt
    carried = zero_block
    grad_img = zero_block
    for cycle_step in range(CYCLE):
        if cycle_step > 0:
            visiting = shifted(visiting, "dp", 1)
            carried = shifted(carried, "dp", 1)
        if cycle_step == 0:
            sign_label = 2.0 * identity_mask - 1.0
        else:
            sign_label = negative_label
        pair_weight = weigh_pairs(
            low_img, visiting, affinity_multiplier_name, shift_value, sign_label
        )
        grad_img = grad_img + jnp.dot(pair_weight, visiting, preferred_element_type=jnp.float32)
        carried = carried + contract_rows(pair_weight, low_img)
    grad_txt = shifted(carried, "dp", 1 - CYCLE)
    img_tangent = (
        norm_img * (grad_img - unit_img * jnp.sum(unit_img * grad_img, axis=1, keepdims=True))
    ).astype(jnp.bfloat16)
    txt_tangent = (
        norm_txt
        * (grad_txt - normalized_text * jnp.sum(normalized_text * grad_txt, axis=1, keepdims=True))
    ).astype(jnp.bfloat16)
    part_img = picture_tower_inputs
    part_txt = caption_tower_inputs
    owned_rows = lax.psum_scatter(
        jnp.concatenate(
            [contract_rows(part_img, img_tangent), contract_rows(part_txt, txt_tangent)], axis=1
        ).astype(jnp.bfloat16),
        "fsdp",
        scatter_dimension=0,
        tiled=True,
    ).astype(jnp.float32)
    gradient = lax.psum_scatter(owned_rows, "dp", scatter_dimension=1, tiled=True)
    new_one = 0.9 * gradient_mean_estimate + 0.1 * gradient
    new_two = 0.95 * gradient_variance_estimate + 0.05 * gradient * gradient
    new_master = precise_parameter_copy - 0.001 * (
        new_one / (jnp.sqrt(new_two) + 1e-08) + 0.1 * precise_parameter_copy
    )
    new_weights = lax.all_gather(new_master.astype(jnp.bfloat16), "dp", axis=1, tiled=True)
    return (img_tangent, txt_tangent, new_master, new_one, new_two, new_weights)


def solution(mesh):
    return jax.shard_map(
        body,
        mesh=mesh,
        in_specs=(
            P(("dp", "fsdp"), None),
            P(("dp", "fsdp"), None),
            P("fsdp", None),
            P(),
            P(),
            P("fsdp", "dp"),
            P("fsdp", "dp"),
            P("fsdp", "dp"),
        ),
        out_specs=(
            P(("dp", "fsdp"), None),
            P(("dp", "fsdp"), None),
            P("fsdp", "dp"),
            P("fsdp", "dp"),
            P("fsdp", "dp"),
            P("fsdp", None),
        ),
        check_vma=False,
    )
```

profile of v0, /device:TPU:4, one launch (start us, length us, event | category | flops | bytes accessed | tf_op | source)
XLA Modules:
  0.0 1053.1 jit_solution(14474370178524340292)
XLA Ops:
  9.3 48.2 %all-gather.4.cloned.1.call-done = bf16[1152,2304]{1,0:T(8,128)(2,1)} async-done(((bf16[288,2304]{1,0:T(8,128)(2,1)}), bf16[1152,2304]{1,0:T(8,128)(2,1)}) %all-gather.4.cloned.1.call-update) | async-done | bytes 5308432 | tf_op jit(solution)/shard_map/all_gather | solution.py:52
  57.5 3.8 multiply_reduce_fusion.3
  61.4 1.9 multiply_reduce_fusion.2
  63.7 1.1 fusion.33
  64.8 0.9 fusion.40
  65.7 2.4 collective-permute-start.3
  68.0 0.9 collective-permute-start
  69.0 80.9 %collective-permute-done = bf16[512,1152]{1,0:T(8,128)(2,1)S(1)} collective-permute-done((bf16[512,1152]{1,0:T(8,128)(2,1)S(1)}, bf16[512,1152]{1,0:T(8,128)(2,1)S(1)}, u32[]{:S(2)}, u32[]{:S(2)}) %collective-permute-start) | collective-permute-done | bytes 1179680 | tf_op jit(solution)/shard_map/ppermute | solution.py:12
  149.9 1.0 fusion.36
  150.9 0.9 convolution_add_fusion
  152.0 82.2 %collective-permute-done.1 = bf16[512,1152]{1,0:T(8,128)(2,1)S(1)} collective-permute-done((bf16[512,1152]{1,0:T(8,128)(2,1)S(1)}, bf16[512,1152]{1,0:T(8,128)(2,1)S(1)}, u32[]{:S(2)}, u32[]{:S(2)}) %collective-permute-start.1) | collective-permute-done | bytes 1179680 | tf_op jit(solution)/shard_map/ppermute | solution.py:12
  234.2 1.0 fusion.35
  235.2 0.9 fusion.41
  236.7 81.4 %collective-permute-done.2 = bf16[512,1152]{1,0:T(8,128)(2,1)S(1)} collective-permute-done((bf16[512,1152]{1,0:T(8,128)(2,1)S(1)}, bf16[512,1152]{1,0:T(8,128)(2,1)S(1)}, u32[]{:S(2)}, u32[]{:S(2)}) %collective-permute-start.2) | collective-permute-done | bytes 1179680 | tf_op jit(solution)/shard_map/ppermute | solution.py:12
  318.1 1.0 fusion.34
  319.1 0.9 fusion.42
  322.9 1.1 multiply_reduce_fusion.1
  324.4 1.7 fusion.1
  326.2 85.0 %collective-permute-done.6 = f32[512,1152]{1,0:T(8,128)S(1)} collective-permute-done((f32[512,1152]{1,0:T(8,128)S(1)}, f32[512,1152]{1,0:T(8,128)S(1)}, u32[]{:S(2)}, u32[]{:S(2)}) %collective-permute-start.6) | collective-permute-done | bytes 2359328 | tf_op jit(solution)/shard_map/ppermute | solution.py:12
  412.0 1.0 copy-done.2
  413.0 1.7 fusion.2
  414.8 2.8 pad_maximum_fusion
  417.5 8.6 copy.17
  426.2 68.9 %reduce-scatter.6.cloned.1.call-done = bf16[288,2304]{1,0:T(8,128)(2,1)} async-done(((bf16[1152,2304]{1,0:T(8,128)(2,1)}), bf16[288,2304]{1,0:T(8,128)(2,1)}) %reduce-scatter.6.cloned.1.call-update) | async-done | bytes 1327120
  495.1 1.9 copy.18
  497.0 2.0 convert_element_type.40
  499.0 187.4 %fusion = f32[288,48]{0,1:T(8,128)S(1)} fusion(f32[288,2304]{0,1:T(8,128)} %convert_element_type.40), kind=kCustom, calls=%all-reduce-scatter | all-reduce-scatter fusion | flops 884737 | bytes 2710528
  686.4 1.3 collective-permute-start.22
  687.7 1.3 collective-permute-start.21
  689.0 1.3 collective-permute-start.20
  690.3 1.3 collective-permute-start.19
  691.6 1.5 collective-permute-start.18
  693.2 1.3 collective-permute-start.17
  694.5 12.9 %collective-permute-start.16 = (f32[288,48]{0,1:T(8,128)S(1)}, f32[288,48]{0,1:T(8,128)S(1)}, u32[]{:S(2)}, u32[]{:S(2)}) collective-permute-start(f32[288,48]{0,1:T(8,128)S(1)} %fusion), channel_id=1, source_target_pairs={{0,40},{4,44},{8,48},{12,52},{16,56},{20,60},{24,64},{28,68},{32,7... | collective-permute-start | bytes 165896
  707.4 2.5 collective-permute-start.15
  710.0 5.2 collective-permute-start.14
  715.2 2.2 collective-permute-start.13
  717.4 3.4 collective-permute-start.12
  720.8 4.0 collective-permute-start.11
  724.8 3.0 collective-permute-start.10
  727.8 3.3 collective-permute-start.9
  731.2 1.4 collective-permute-start.8
  732.6 4.0 collective-permute-start.7
  738.0 4.1 concatenate.5
  742.1 1.6 convert_bitcast_fusion
  743.7 298.5 %all-gather.6.cloned.1.call-done = bf16[64,36,288]{2,1,0:T(8,128)(2,1)} async-done(((bf16[1,36,288]{2,1,0:T(8,128)(2,1)}), bf16[64,36,288]{2,1,0:T(8,128)(2,1)}) %all-gather.6.cloned.1.call-update) | async-done | bytes 1327120 | tf_op jit(solution)/shard_map/all_gather | solution.py:109
  1042.2 2.8 reshape.27
  1045.0 1.6 copy.16
  (57 shorter events, 6.8 us)
Async XLA Ops:
  7.2 50.3 %copy-start = (bf16[512,1152]{1,0:T(8,128)(2,1)S(1)}, bf16[512,1152]{1,0:T(8,128)(2,1)}, u32[]{:S(2)}) copy-start(bf16[512,1152]{1,0:T(8,128)(2,1)} %param.8) | copy-start | bytes 3538948
  7.2 50.3 %all-gather.4.cloned.1.call-start = ((), (), s32[]{:S(2)}) async-start(), calls=%async_computation.1 | async-start | bytes 6635520 | tf_op jit(solution)/shard_map/all_gather | solution.py:52
  7.9 487.1 %reduce-scatter.6.cloned.1.call-start = ((), (), s32[]{:S(2)}) async-start(), calls=%async_computation.3 | async-start | bytes 6635520
  9.3 52.1 %copy-start.6 = (bf16[512,1152]{1,0:T(8,128)(2,1)S(1)}, bf16[512,1152]{1,0:T(8,128)(2,1)}, u32[]{:S(2)}) copy-start(bf16[512,1152]{1,0:T(8,128)(2,1)} %param.9) | copy-start | bytes 3538948
  57.5 3.9 copy-start.5
  65.7 85.2 %collective-permute-start.3 = (f32[512,1152]{1,0:T(8,128)S(1)}, f32[512,1152]{1,0:T(8,128)S(1)}, u32[]{:S(2)}, u32[]{:S(2)}) collective-permute-start(f32[512,1152]{1,0:T(8,128)S(1)} %fusion.40), channel_id=1, source_target_pairs={{0,4},{4,8},{8,12},{12,16},{16,20},{20,24},{24,28},{28,32},{32,36}... | collective-permute-start | bytes 7077896 | tf_op jit(solution)/shard_map/ppermute | solution.py:12
  68.0 81.9 %collective-permute-start = (bf16[512,1152]{1,0:T(8,128)(2,1)S(1)}, bf16[512,1152]{1,0:T(8,128)(2,1)S(1)}, u32[]{:S(2)}, u32[]{:S(2)}) collective-permute-start(bf16[512,1152]{1,0:T(8,128)(2,1)S(1)} %multiply_convert_fusion.2), channel_id=1, source_target_pairs={{0,4},{4,8},{8,12},{12,16},{16,20},{20,24},{24,28},{28,32},{32,36}... | collective-permute-start | bytes 3538952 | tf_op jit(solution)/shard_map/ppermute | solution.py:12
  151.8 84.3 %collective-permute-start.4 = (f32[512,1152]{1,0:T(8,128)S(1)}, f32[512,1152]{1,0:T(8,128)S(1)}, u32[]{:S(2)}, u32[]{:S(2)}) collective-permute-start(f32[512,1152]{1,0:T(8,128)S(1)} %convolution_add_fusion), channel_id=1, source_target_pairs={{0,4},{4,8},{8,12},{12,16},{16,20},{20,24},{24,28},{28,32},{32,36}... | collective-permute-start | bytes 7077896 | tf_op jit(solution)/shard_map/ppermute | solution.py:12
  151.9 82.3 %collective-permute-start.1 = (bf16[512,1152]{1,0:T(8,128)(2,1)S(1)}, bf16[512,1152]{1,0:T(8,128)(2,1)S(1)}, u32[]{:S(2)}, u32[]{:S(2)}) collective-permute-start(bf16[512,1152]{1,0:T(8,128)(2,1)S(1)} %collective-permute-done), channel_id=1, source_target_pairs={{0,4},{4,8},{8,12},{12,16},{16,20},{20,24},{24,28},{28,32},{32,36}... | collective-permute-start | bytes 3538952 | tf_op jit(solution)/shard_map/ppermute | solution.py:12
  236.4 83.6 %collective-permute-start.5 = (f32[512,1152]{1,0:T(8,128)S(1)}, f32[512,1152]{1,0:T(8,128)S(1)}, u32[]{:S(2)}, u32[]{:S(2)}) collective-permute-start(f32[512,1152]{1,0:T(8,128)S(1)} %add.99), channel_id=1, source_target_pairs={{0,4},{4,8},{8,12},{12,16},{16,20},{20,24},{24,28},{28,32},{32,36}... | collective-permute-start | bytes 7077896 | tf_op jit(solution)/shard_map/ppermute | solution.py:12
  236.6 81.5 %collective-permute-start.2 = (bf16[512,1152]{1,0:T(8,128)(2,1)S(1)}, bf16[512,1152]{1,0:T(8,128)(2,1)S(1)}, u32[]{:S(2)}, u32[]{:S(2)}) collective-permute-start(bf16[512,1152]{1,0:T(8,128)(2,1)S(1)} %collective-permute-done.1), channel_id=1, source_target_pairs={{0,4},{4,8},{8,12},{12,16},{16,20},{20,24},{24,28},{28,32},{32,36}... | collective-permute-start | bytes 3538952 | tf_op jit(solution)/shard_map/ppermute | solution.py:12
  320.2 91.0 %collective-permute-start.6 = (f32[512,1152]{1,0:T(8,128)S(1)}, f32[512,1152]{1,0:T(8,128)S(1)}, u32[]{:S(2)}, u32[]{:S(2)}) collective-permute-start(f32[512,1152]{1,0:T(8,128)S(1)} %add.100), channel_id=1, source_target_pairs={{0,244},{4,248},{8,252},{12,0},{16,4},{20,8},{24,12},{28,16},{32,2... | collective-permute-start | bytes 7077896 | tf_op jit(solution)/shard_map/ppermute | solution.py:12
  324.4 1.8 copy-start.1
  412.0 1.0 copy-start.2
  426.1 616.1 %all-gather.6.cloned.1.call-start = ((), (), s32[]{:S(2)}) async-start(), calls=%async_computation.2 | async-start | bytes 1996800 | tf_op jit(solution)/shard_map/all_gather | solution.py:109
  499.0 237.7 %copy-start.4 = (u32[256]{0:T(256)S(1)}, u32[256]{0:T(256)}, u32[]{:S(2)}) copy-start(u32[256]{0:T(256)} %constant.28) | copy-start | bytes 3076
  686.4 6.7 collective-permute-start.22
  687.7 6.8 collective-permute-start.21
  689.0 18.4 %collective-permute-start.20 = (f32[288,48]{0,1:T(8,128)S(1)}, f32[288,48]{0,1:T(8,128)S(1)}, u32[]{:S(2)}, u32[]{:S(2)}) collective-permute-start(f32[288,48]{0,1:T(8,128)S(1)} %fusion), channel_id=1, source_target_pairs={{0,56},{4,60},{8,64},{12,68},{16,72},{20,76},{24,80},{28,84},{32,8... | collective-permute-start | bytes 165896
  690.3 19.6 %collective-permute-start.19 = (f32[288,48]{0,1:T(8,128)S(1)}, f32[288,48]{0,1:T(8,128)S(1)}, u32[]{:S(2)}, u32[]{:S(2)}) collective-permute-start(f32[288,48]{0,1:T(8,128)S(1)} %fusion), channel_id=1, source_target_pairs={{0,52},{4,56},{8,60},{12,64},{16,68},{20,72},{24,76},{28,80},{32,8... | collective-permute-start | bytes 165896
  691.6 23.5 %collective-permute-start.18 = (f32[288,48]{0,1:T(8,128)S(1)}, f32[288,48]{0,1:T(8,128)S(1)}, u32[]{:S(2)}, u32[]{:S(2)}) collective-permute-start(f32[288,48]{0,1:T(8,128)S(1)} %fusion), channel_id=1, source_target_pairs={{0,48},{4,52},{8,56},{12,60},{16,64},{20,68},{24,72},{28,76},{32,8... | collective-permute-start | bytes 165896
  693.1 39.5 %copy-start.3 = (f32[288,36]{0,1:T(8,128)}, f32[288,36]{0,1:T(8,128)S(1)}, u32[]{:S(2)}) copy-start(f32[288,36]{0,1:T(8,128)S(1)} %collective-permute-done.22) | copy-start | bytes 124420
  693.2 24.2 %collective-permute-start.17 = (f32[288,48]{0,1:T(8,128)S(1)}, f32[288,48]{0,1:T(8,128)S(1)}, u32[]{:S(2)}, u32[]{:S(2)}) collective-permute-start(f32[288,48]{0,1:T(8,128)S(1)} %fusion), channel_id=1, source_target_pairs={{0,44},{4,48},{8,52},{12,56},{16,60},{20,64},{24,68},{28,72},{32,7... | collective-permute-start | bytes 165896
  694.5 26.3 %collective-permute-start.16 = (f32[288,48]{0,1:T(8,128)S(1)}, f32[288,48]{0,1:T(8,128)S(1)}, u32[]{:S(2)}, u32[]{:S(2)}) collective-permute-start(f32[288,48]{0,1:T(8,128)S(1)} %fusion), channel_id=1, source_target_pairs={{0,40},{4,44},{8,48},{12,52},{16,56},{20,60},{24,64},{28,68},{32,7... | collective-permute-start | bytes 165896
  707.4 17.4 %collective-permute-start.15 = (f32[288,48]{0,1:T(8,128)S(1)}, f32[288,48]{0,1:T(8,128)S(1)}, u32[]{:S(2)}, u32[]{:S(2)}) collective-permute-start(f32[288,48]{0,1:T(8,128)S(1)} %fusion), channel_id=1, source_target_pairs={{0,36},{4,40},{8,44},{12,48},{16,52},{20,56},{24,60},{28,64},{32,6... | collective-permute-start | bytes 165896
  710.0 17.9 %collective-permute-start.14 = (f32[288,48]{0,1:T(8,128)S(1)}, f32[288,48]{0,1:T(8,128)S(1)}, u32[]{:S(2)}, u32[]{:S(2)}) collective-permute-start(f32[288,48]{0,1:T(8,128)S(1)} %fusion), channel_id=1, source_target_pairs={{0,32},{4,36},{8,40},{12,44},{16,48},{20,52},{24,56},{28,60},{32,6... | collective-permute-start | bytes 165896
  715.2 16.0 %collective-permute-start.13 = (f32[288,48]{0,1:T(8,128)S(1)}, f32[288,48]{0,1:T(8,128)S(1)}, u32[]{:S(2)}, u32[]{:S(2)}) collective-permute-start(f32[288,48]{0,1:T(8,128)S(1)} %fusion), channel_id=1, source_target_pairs={{0,28},{4,32},{8,36},{12,40},{16,44},{20,48},{24,52},{28,56},{32,6... | collective-permute-start | bytes 165896
  717.4 15.2 %collective-permute-start.12 = (f32[288,48]{0,1:T(8,128)S(1)}, f32[288,48]{0,1:T(8,128)S(1)}, u32[]{:S(2)}, u32[]{:S(2)}) collective-permute-start(f32[288,48]{0,1:T(8,128)S(1)} %fusion), channel_id=1, source_target_pairs={{0,24},{4,28},{8,32},{12,36},{16,40},{20,44},{24,48},{28,52},{32,5... | collective-permute-start | bytes 165896
  720.8 17.1 %collective-permute-start.11 = (f32[288,48]{0,1:T(8,128)S(1)}, f32[288,48]{0,1:T(8,128)S(1)}, u32[]{:S(2)}, u32[]{:S(2)}) collective-permute-start(f32[288,48]{0,1:T(8,128)S(1)} %fusion), channel_id=1, source_target_pairs={{0,20},{4,24},{8,28},{12,32},{16,36},{20,40},{24,44},{28,48},{32,5... | collective-permute-start | bytes 165896
  724.8 13.1 %collective-permute-start.10 = (f32[288,48]{0,1:T(8,128)S(1)}, f32[288,48]{0,1:T(8,128)S(1)}, u32[]{:S(2)}, u32[]{:S(2)}) collective-permute-start(f32[288,48]{0,1:T(8,128)S(1)} %fusion), channel_id=1, source_target_pairs={{0,16},{4,20},{8,24},{12,28},{16,32},{20,36},{24,40},{28,44},{32,4... | collective-permute-start | bytes 165896
  727.8 10.1 collective-permute-start.9
  731.2 6.7 collective-permute-start.8
  732.6 5.3 collective-permute-start.7
Sparse Core Ops, SparseCore 0:
  9.8 47.6 all-gather.3
  426.2 68.7 reduce-scatter.5
  743.8 298.3 all-gather.5
where the time goes:
time: 1050 us
  waiting for transfers between devices  746 us (71%)
  blocking collectives  187 us (18%)
  starting transfers between devices  54 us (5%)
  local copies, waits for them, and re-layouts  20.6 us (2%)
  matrix products  20.5 us (2%)
  between operations  16.3 us (2%)
    ppermute x7, waiting for transfers between devices, shifted(): return lax.ppermute(value, axis, pairs)  329 us
    all_gather x1, waiting for transfers between devices, body(): lax.all_gather(new_master.astype(jnp.bfloat16), 'dp', axis=1, tiled=True)  299 us
    unnamed x1, blocking collectives  187 us
    unnamed x20, waiting for transfers between devices  69.7 us
    unnamed x17, starting transfers between devices  50 us
    all_gather x1, waiting for transfers between devices, body(): lax.all_gather(halfwidth_parameter_matrix, 'fsdp', axis=0, tiled=True)  48.2 us
  transfers between devices with their start and end apart: 26, of which 8 were waited for; matrix products, arithmetic and copies ran while one was open for 1% of the time, Pallas kernels for 0%

commit v1 on v0

--- a/solution.py
+++ b/solution.py
@@ -106,7 +106,14 @@
     new_master = precise_parameter_copy - 0.001 * (
         new_one / (jnp.sqrt(new_two) + 1e-08) + 0.1 * precise_parameter_copy
     )
-    new_weights = lax.all_gather(new_master.astype(jnp.bfloat16), "dp", axis=1, tiled=True)
+
+    def pair_the_target(array_here):
+        arr_now = jnp.concatenate(
+            lax.all_to_all(jnp.stack(lax.axis_size("dp") * [array_here]), "dp", 0, 0), 1
+        )
+        return arr_now
+
+    new_weights = pair_the_target(new_master.astype(jnp.bfloat16))
     return (img_tangent, txt_tangent, new_master, new_one, new_two, new_weights)
 
 

time: 1050 us -> 803 us (0.76)
  waiting for transfers between devices: 746 us -> 448 us
  blocking collectives: 187 us -> 232 us
    all_gather x1 -> x0, waiting for transfers between devices: 299 us -> none  [body(): lax.all_gather(new_master.astype(jnp.bfloat16), 'dp', axis=1, tiled=True)]
    all_to_all x0 -> x1, blocking collectives: none -> 43.8 us  [pair_the_target(): lax.all_to_all(jnp.stack(lax.axis_size('dp') * [array_here]), 'dp', 0, 0)]
    unnamed x20 -> x19, waiting for transfers between devices: 69.7 us -> 70.2 us
  transfers between devices with their start and end apart: 26 -> 25, of which waited for: 8 -> 7; matrix products, arithmetic and copies ran while one was open for 1% -> 1% of each run, Pallas kernels for 0% -> 0%
where the time goes in v1:
time: 803 us; the launch traced here: 800 us
  waiting for transfers between devices  448 us (56%)
  blocking collectives  232 us (29%)
  starting transfers between devices  54.2 us (7%)
  local copies, waits for them, and re-layouts  20.7 us (3%)
  matrix products  20.5 us (3%)
  between operations  16.5 us (2%)
  other arithmetic  8.5 us (1%)
    ppermute x7, waiting for transfers between devices, shifted(): return lax.ppermute(value, axis, pairs)  330 us
    unnamed x1, blocking collectives  188 us
    unnamed x19, waiting for transfers between devices  70.2 us
    unnamed x17, starting transfers between devices  50.2 us
    all_gather x1, waiting for transfers between devices, body(): lax.all_gather(halfwidth_parameter_matrix, 'fsdp', axis=0, tiled=True)  48.2 us
    all_to_all x1, blocking collectives, pair_the_target(): lax.all_to_all(jnp.stack(lax.axis_size('dp') * [array_here]), 'dp', 0, 0)  43.8 us
    unnamed x20, local copies, waits for them, and re-layouts  18.8 us
  transfers between devices with their start and end apart: 25, of which 7 were waited for; matrix products, arithmetic and copies ran while one was open for 1% of the time, Pallas kernels for 0%

profile of v1, /device:TPU:4, one launch (start us, length us, event | category | flops | bytes accessed | tf_op | source)
XLA Modules:
  0.0 800.4 jit_solution(4183265258245417102)
XLA Ops:
  9.3 48.2 %all-gather.2.cloned.1.call-done = bf16[1152,2304]{1,0:T(8,128)(2,1)} async-done(((bf16[288,2304]{1,0:T(8,128)(2,1)}), bf16[1152,2304]{1,0:T(8,128)(2,1)}) %all-gather.2.cloned.1.call-update) | async-done | bytes 5308432 | tf_op jit(solution)/shard_map/all_gather | solution.py:52
  57.5 3.8 multiply_reduce_fusion.3
  61.4 1.9 multiply_reduce_fusion.2
  63.7 1.1 fusion.33
  64.8 0.9 fusion.41
  65.7 2.4 collective-permute-start.3
  68.0 0.9 collective-permute-start
  69.0 80.9 %collective-permute-done = bf16[512,1152]{1,0:T(8,128)(2,1)S(1)} collective-permute-done((bf16[512,1152]{1,0:T(8,128)(2,1)S(1)}, bf16[512,1152]{1,0:T(8,128)(2,1)S(1)}, u32[]{:S(2)}, u32[]{:S(2)}) %collective-permute-start) | collective-permute-done | bytes 1179680 | tf_op jit(solution)/shard_map/ppermute | solution.py:12
  149.9 1.0 fusion.36
  150.9 0.9 convolution_add_fusion
  152.0 82.2 %collective-permute-done.1 = bf16[512,1152]{1,0:T(8,128)(2,1)S(1)} collective-permute-done((bf16[512,1152]{1,0:T(8,128)(2,1)S(1)}, bf16[512,1152]{1,0:T(8,128)(2,1)S(1)}, u32[]{:S(2)}, u32[]{:S(2)}) %collective-permute-start.1) | collective-permute-done | bytes 1179680 | tf_op jit(solution)/shard_map/ppermute | solution.py:12
  234.2 1.0 fusion.35
  235.2 0.9 fusion.42
  236.7 81.4 %collective-permute-done.2 = bf16[512,1152]{1,0:T(8,128)(2,1)S(1)} collective-permute-done((bf16[512,1152]{1,0:T(8,128)(2,1)S(1)}, bf16[512,1152]{1,0:T(8,128)(2,1)S(1)}, u32[]{:S(2)}, u32[]{:S(2)}) %collective-permute-start.2) | collective-permute-done | bytes 1179680 | tf_op jit(solution)/shard_map/ppermute | solution.py:12
  318.1 1.0 fusion.34
  319.1 0.9 fusion.43
  322.9 1.1 multiply_reduce_fusion.1
  324.4 1.7 fusion.1
  326.2 85.0 %collective-permute-done.6 = f32[512,1152]{1,0:T(8,128)S(1)} collective-permute-done((f32[512,1152]{1,0:T(8,128)S(1)}, f32[512,1152]{1,0:T(8,128)S(1)}, u32[]{:S(2)}, u32[]{:S(2)}) %collective-permute-start.6) | collective-permute-done | bytes 2359328 | tf_op jit(solution)/shard_map/ppermute | solution.py:12
  412.0 1.0 copy-done.2
  413.0 1.7 fusion.2
  414.8 2.8 pad_maximum_fusion
  417.6 8.6 %copy.17 = bf16[1152,2304]{1,0:T(8,128)(2,1)} copy(bf16[1152,2304]{0,1:T(8,128)(2,1)} %pad_maximum_fusion) | data formatting | bytes 10616832
  426.1 68.9 %reduce-scatter.6.cloned.1.call-done = bf16[288,2304]{1,0:T(8,128)(2,1)} async-done(((bf16[1152,2304]{1,0:T(8,128)(2,1)}), bf16[288,2304]{1,0:T(8,128)(2,1)}) %reduce-scatter.6.cloned.1.call-update) | async-done | bytes 1327120
  495.1 1.9 copy.18
  497.0 2.0 convert_element_type.40
  499.0 188.3 %fusion = f32[288,48]{0,1:T(8,128)S(1)} fusion(f32[288,2304]{0,1:T(8,128)} %convert_element_type.40), kind=kCustom, calls=%all-reduce-scatter | all-reduce-scatter fusion | flops 884737 | bytes 2710528
  687.3 1.3 collective-permute-start.22
  688.6 1.3 collective-permute-start.21
  690.0 1.3 collective-permute-start.20
  691.3 1.3 collective-permute-start.19
  692.6 1.5 collective-permute-start.18
  694.1 1.3 collective-permute-start.17
  695.4 12.9 %collective-permute-start.16 = (f32[288,48]{0,1:T(8,128)S(1)}, f32[288,48]{0,1:T(8,128)S(1)}, u32[]{:S(2)}, u32[]{:S(2)}) collective-permute-start(f32[288,48]{0,1:T(8,128)S(1)} %fusion), channel_id=1, source_target_pairs={{0,40},{4,44},{8,48},{12,52},{16,56},{20,60},{24,64},{28,68},{32,7... | collective-permute-start | bytes 165896
  708.3 2.5 collective-permute-start.15
  710.9 5.4 collective-permute-start.14
  716.3 2.0 collective-permute-start.13
  718.3 3.6 collective-permute-start.12
  721.9 3.8 collective-permute-start.11
  725.7 3.0 collective-permute-start.10
  728.8 3.3 collective-permute-start.9
  732.1 1.4 collective-permute-start.8
  733.6 4.2 collective-permute-start.7
  739.6 4.1 concatenate.5
  743.7 1.6 fusion.38
  745.4 43.8 %all_to_all.5 = bf16[64,288,36]{1,2,0:T(8,128)(2,1)S(1)} all-to-all(bf16[64,288,36]{1,2,0:T(8,128)(2,1)S(1)} %stack.2), channel_id=1, replica_groups=mesh['dp'=64,'fsdp'=4] {'dp'}, dimensions={0} | all-to-all | bytes 2654208 | tf_op jit(solution)/shard_map/all_to_all | solution.py:112
  789.3 1.8 reshape.35
  791.0 2.6 copy.16
  (56 shorter events, 7.4 us)
Async XLA Ops:
  7.2 50.3 %copy-start = (bf16[512,1152]{1,0:T(8,128)(2,1)S(1)}, bf16[512,1152]{1,0:T(8,128)(2,1)}, u32[]{:S(2)}) copy-start(bf16[512,1152]{1,0:T(8,128)(2,1)} %param.8) | copy-start | bytes 3538948
  7.2 50.3 %all-gather.2.cloned.1.call-start = ((), (), s32[]{:S(2)}) async-start(), calls=%async_computation.2 | async-start | bytes 6635520 | tf_op jit(solution)/shard_map/all_gather | solution.py:52
  7.9 487.2 %reduce-scatter.6.cloned.1.call-start = ((), (), s32[]{:S(2)}) async-start(), calls=%async_computation.3 | async-start | bytes 6635520
  9.3 52.1 %copy-start.6 = (bf16[512,1152]{1,0:T(8,128)(2,1)S(1)}, bf16[512,1152]{1,0:T(8,128)(2,1)}, u32[]{:S(2)}) copy-start(bf16[512,1152]{1,0:T(8,128)(2,1)} %param.9) | copy-start | bytes 3538948
  57.5 3.9 copy-start.5
  65.7 85.2 %collective-permute-start.3 = (f32[512,1152]{1,0:T(8,128)S(1)}, f32[512,1152]{1,0:T(8,128)S(1)}, u32[]{:S(2)}, u32[]{:S(2)}) collective-permute-start(f32[512,1152]{1,0:T(8,128)S(1)} %fusion.41), channel_id=1, source_target_pairs={{0,4},{4,8},{8,12},{12,16},{16,20},{20,24},{24,28},{28,32},{32,36}... | collective-permute-start | bytes 7077896 | tf_op jit(solution)/shard_map/ppermute | solution.py:12
  68.0 81.9 %collective-permute-start = (bf16[512,1152]{1,0:T(8,128)(2,1)S(1)}, bf16[512,1152]{1,0:T(8,128)(2,1)S(1)}, u32[]{:S(2)}, u32[]{:S(2)}) collective-permute-start(bf16[512,1152]{1,0:T(8,128)(2,1)S(1)} %multiply_convert_fusion.2), channel_id=1, source_target_pairs={{0,4},{4,8},{8,12},{12,16},{16,20},{20,24},{24,28},{28,32},{32,36}... | collective-permute-start | bytes 3538952 | tf_op jit(solution)/shard_map/ppermute | solution.py:12
  151.8 84.3 %collective-permute-start.4 = (f32[512,1152]{1,0:T(8,128)S(1)}, f32[512,1152]{1,0:T(8,128)S(1)}, u32[]{:S(2)}, u32[]{:S(2)}) collective-permute-start(f32[512,1152]{1,0:T(8,128)S(1)} %convolution_add_fusion), channel_id=1, source_target_pairs={{0,4},{4,8},{8,12},{12,16},{16,20},{20,24},{24,28},{28,32},{32,36}... | collective-permute-start | bytes 7077896 | tf_op jit(solution)/shard_map/ppermute | solution.py:12
  151.9 82.3 %collective-permute-start.1 = (bf16[512,1152]{1,0:T(8,128)(2,1)S(1)}, bf16[512,1152]{1,0:T(8,128)(2,1)S(1)}, u32[]{:S(2)}, u32[]{:S(2)}) collective-permute-start(bf16[512,1152]{1,0:T(8,128)(2,1)S(1)} %collective-permute-done), channel_id=1, source_target_pairs={{0,4},{4,8},{8,12},{12,16},{16,20},{20,24},{24,28},{28,32},{32,36}... | collective-permute-start | bytes 3538952 | tf_op jit(solution)/shard_map/ppermute | solution.py:12
  236.4 83.6 %collective-permute-start.5 = (f32[512,1152]{1,0:T(8,128)S(1)}, f32[512,1152]{1,0:T(8,128)S(1)}, u32[]{:S(2)}, u32[]{:S(2)}) collective-permute-start(f32[512,1152]{1,0:T(8,128)S(1)} %add.99), channel_id=1, source_target_pairs={{0,4},{4,8},{8,12},{12,16},{16,20},{20,24},{24,28},{28,32},{32,36}... | collective-permute-start | bytes 7077896 | tf_op jit(solution)/shard_map/ppermute | solution.py:12
  236.6 81.5 %collective-permute-start.2 = (bf16[512,1152]{1,0:T(8,128)(2,1)S(1)}, bf16[512,1152]{1,0:T(8,128)(2,1)S(1)}, u32[]{:S(2)}, u32[]{:S(2)}) collective-permute-start(bf16[512,1152]{1,0:T(8,128)(2,1)S(1)} %collective-permute-done.1), channel_id=1, source_target_pairs={{0,4},{4,8},{8,12},{12,16},{16,20},{20,24},{24,28},{28,32},{32,36}... | collective-permute-start | bytes 3538952 | tf_op jit(solution)/shard_map/ppermute | solution.py:12
  320.2 91.0 %collective-permute-start.6 = (f32[512,1152]{1,0:T(8,128)S(1)}, f32[512,1152]{1,0:T(8,128)S(1)}, u32[]{:S(2)}, u32[]{:S(2)}) collective-permute-start(f32[512,1152]{1,0:T(8,128)S(1)} %add.100), channel_id=1, source_target_pairs={{0,244},{4,248},{8,252},{12,0},{16,4},{20,8},{24,12},{28,16},{32,2... | collective-permute-start | bytes 7077896 | tf_op jit(solution)/shard_map/ppermute | solution.py:12
  324.4 1.8 copy-start.1
  412.0 1.0 copy-start.2
  499.0 238.8 %copy-start.4 = (u32[256]{0:T(256)S(1)}, u32[256]{0:T(256)}, u32[]{:S(2)}) copy-start(u32[256]{0:T(256)} %constant.28) | copy-start | bytes 3076
  687.3 6.7 collective-permute-start.22
  688.6 6.8 collective-permute-start.21
  690.0 18.4 %collective-permute-start.20 = (f32[288,48]{0,1:T(8,128)S(1)}, f32[288,48]{0,1:T(8,128)S(1)}, u32[]{:S(2)}, u32[]{:S(2)}) collective-permute-start(f32[288,48]{0,1:T(8,128)S(1)} %fusion), channel_id=1, source_target_pairs={{0,56},{4,60},{8,64},{12,68},{16,72},{20,76},{24,80},{28,84},{32,8... | collective-permute-start | bytes 165896
  691.3 19.6 %collective-permute-start.19 = (f32[288,48]{0,1:T(8,128)S(1)}, f32[288,48]{0,1:T(8,128)S(1)}, u32[]{:S(2)}, u32[]{:S(2)}) collective-permute-start(f32[288,48]{0,1:T(8,128)S(1)} %fusion), channel_id=1, source_target_pairs={{0,52},{4,56},{8,60},{12,64},{16,68},{20,72},{24,76},{28,80},{32,8... | collective-permute-start | bytes 165896
  692.6 23.8 %collective-permute-start.18 = (f32[288,48]{0,1:T(8,128)S(1)}, f32[288,48]{0,1:T(8,128)S(1)}, u32[]{:S(2)}, u32[]{:S(2)}) collective-permute-start(f32[288,48]{0,1:T(8,128)S(1)} %fusion), channel_id=1, source_target_pairs={{0,48},{4,52},{8,56},{12,60},{16,64},{20,68},{24,72},{28,76},{32,8... | collective-permute-start | bytes 165896
  694.1 39.5 %copy-start.3 = (f32[288,36]{0,1:T(8,128)}, f32[288,36]{0,1:T(8,128)S(1)}, u32[]{:S(2)}) copy-start(f32[288,36]{0,1:T(8,128)S(1)} %collective-permute-done.22) | copy-start | bytes 124420
  694.1 24.2 %collective-permute-start.17 = (f32[288,48]{0,1:T(8,128)S(1)}, f32[288,48]{0,1:T(8,128)S(1)}, u32[]{:S(2)}, u32[]{:S(2)}) collective-permute-start(f32[288,48]{0,1:T(8,128)S(1)} %fusion), channel_id=1, source_target_pairs={{0,44},{4,48},{8,52},{12,56},{16,60},{20,64},{24,68},{28,72},{32,7... | collective-permute-start | bytes 165896
  695.4 26.5 %collective-permute-start.16 = (f32[288,48]{0,1:T(8,128)S(1)}, f32[288,48]{0,1:T(8,128)S(1)}, u32[]{:S(2)}, u32[]{:S(2)}) collective-permute-start(f32[288,48]{0,1:T(8,128)S(1)} %fusion), channel_id=1, source_target_pairs={{0,40},{4,44},{8,48},{12,52},{16,56},{20,60},{24,64},{28,68},{32,7... | collective-permute-start | bytes 165896
  708.3 17.4 %collective-permute-start.15 = (f32[288,48]{0,1:T(8,128)S(1)}, f32[288,48]{0,1:T(8,128)S(1)}, u32[]{:S(2)}, u32[]{:S(2)}) collective-permute-start(f32[288,48]{0,1:T(8,128)S(1)} %fusion), channel_id=1, source_target_pairs={{0,36},{4,40},{8,44},{12,48},{16,52},{20,56},{24,60},{28,64},{32,6... | collective-permute-start | bytes 165896
  710.9 17.9 %collective-permute-start.14 = (f32[288,48]{0,1:T(8,128)S(1)}, f32[288,48]{0,1:T(8,128)S(1)}, u32[]{:S(2)}, u32[]{:S(2)}) collective-permute-start(f32[288,48]{0,1:T(8,128)S(1)} %fusion), channel_id=1, source_target_pairs={{0,32},{4,36},{8,40},{12,44},{16,48},{20,52},{24,56},{28,60},{32,6... | collective-permute-start | bytes 165896
  716.3 15.8 %collective-permute-start.13 = (f32[288,48]{0,1:T(8,128)S(1)}, f32[288,48]{0,1:T(8,128)S(1)}, u32[]{:S(2)}, u32[]{:S(2)}) collective-permute-start(f32[288,48]{0,1:T(8,128)S(1)} %fusion), channel_id=1, source_target_pairs={{0,28},{4,32},{8,36},{12,40},{16,44},{20,48},{24,52},{28,56},{32,6... | collective-permute-start | bytes 165896
  718.3 15.2 %collective-permute-start.12 = (f32[288,48]{0,1:T(8,128)S(1)}, f32[288,48]{0,1:T(8,128)S(1)}, u32[]{:S(2)}, u32[]{:S(2)}) collective-permute-start(f32[288,48]{0,1:T(8,128)S(1)} %fusion), channel_id=1, source_target_pairs={{0,24},{4,28},{8,32},{12,36},{16,40},{20,44},{24,48},{28,52},{32,5... | collective-permute-start | bytes 165896
  721.9 17.1 %collective-permute-start.11 = (f32[288,48]{0,1:T(8,128)S(1)}, f32[288,48]{0,1:T(8,128)S(1)}, u32[]{:S(2)}, u32[]{:S(2)}) collective-permute-start(f32[288,48]{0,1:T(8,128)S(1)} %fusion), channel_id=1, source_target_pairs={{0,20},{4,24},{8,28},{12,32},{16,36},{20,40},{24,44},{28,48},{32,5... | collective-permute-start | bytes 165896
  725.7 13.3 %collective-permute-start.10 = (f32[288,48]{0,1:T(8,128)S(1)}, f32[288,48]{0,1:T(8,128)S(1)}, u32[]{:S(2)}, u32[]{:S(2)}) collective-permute-start(f32[288,48]{0,1:T(8,128)S(1)} %fusion), channel_id=1, source_target_pairs={{0,16},{4,20},{8,24},{12,28},{16,32},{20,36},{24,40},{28,44},{32,4... | collective-permute-start | bytes 165896
  728.8 10.3 %collective-permute-start.9 = (f32[288,48]{0,1:T(8,128)S(1)}, f32[288,48]{0,1:T(8,128)S(1)}, u32[]{:S(2)}, u32[]{:S(2)}) collective-permute-start(f32[288,48]{0,1:T(8,128)S(1)} %fusion), channel_id=1, source_target_pairs={{0,12},{4,16},{8,20},{12,24},{16,28},{20,32},{24,36},{28,40},{32,4... | collective-permute-start | bytes 165896
  732.1 6.9 collective-permute-start.8
  733.6 6.0 collective-permute-start.7
Sparse Core Ops, SparseCore 0:
  9.8 47.6 all-gather.1
  426.3 68.7 reduce-scatter.5
